TPU v7x, 512 devices: a whole 4x4x16 slice. The times are simulated.
512 devices in a mesh: grp: 64 (over z, y), seq: 8 (over x, core).
Axes of the slice: x: 4, y: 4, z: 16, core: 2. Of those that a mesh axis runs over, the one named last changes fastest.
Arguments:
- tokens: bfloat16 [64, 1024, 2048], P('grp', 'seq'), may hold values from -6 to 6
- seg_ids: int32 [64, 1024], P('grp'), may hold values from 0 to 3, never falling along the last dimension, each value on 1 to 512 neighbouring positions
- deal: int32 [64, 1024], P('grp'), may hold values from 0 to 1023, each once within a row
- page_table: int32 [64, 128], P('grp'), may hold values from 0 to 127, each once within a row
- in_gain: float32 [2048], replicated, may hold values from 0.1 to 1.9
- w_query: bfloat16 [2048, 2048], P('grp', 'seq'), may hold values from -0.125 to 0.125
- key_projection_weight: bfloat16 [2048, 512], P('grp'), may hold values from -0.125 to 0.125
- value_projection_weight: bfloat16 [2048, 512], P('grp'), may hold values from -0.125 to 0.125
- q_gain: float32 [256], replicated, may hold values from 1.25 to 3.75
- key_norm_gain: float32 [256], replicated, may hold values from 0.1 to 1.9
- w_out: bfloat16 [2048, 2048], P('seq', 'grp'), may hold values from -0.125 to 0.125
- post_gain: float32 [2048], replicated, may hold values from 0.1 to 1.9
- final_gain: float32 [2048], replicated, may hold values from 0.1 to 1.9
- embed: bfloat16 [262144, 2048], P(('grp', 'seq')), may hold values from -0.375 to 0.375
Outputs:
- hidden_out: bfloat16 [64, 1024, 2048], P('grp', 'seq')
- kv_cache: bfloat16 [64, 128, 8, 1024], P('grp', 'seq')
- last_norm: float32 [256], replicated
- max_logit: float32 [256], replicated
Inputs may be any that keep to these rules, and one draw needn't show every extreme that they name: `seg_ids`: along each pack the prompt numbers never fall; every one of the 4 prompts occurs, none has more than 512 positions, and one has exactly that many. Each row of deal holds every packed position once. Each row of page_table holds every page of the pack once.
All inputs are finite; a program needn't handle non-finite values.
Results may differ from a plain program's by a relative error of at most 0.015.
The roundings to bfloat16 on the way count: a program that leaves them out, or rounds other values in their place, can miss the bound.
Values may be sent and summed in bfloat16 or wider, within the bound.
A program may use at most 64 MiB of HBM per device.

v0:
```python
import jax
import jax.numpy as jnp
from jax import lax
from jax.sharding import PartitionSpec as P

QUERY_HEADS = 8
KEY_HEADS = 2
PAGE_SLOTS = 8
SEGS = 4
eps = 1e-06
rope_base = 1000000.0
cap_value = 30.0


def rows_scaled(value_rows, scales):
    mean_square = jnp.mean(value_rows * value_rows, axis=-1, keepdims=True)
    return value_rows * lax.rsqrt(mean_square + eps) * scales


def rotate(value_rows, offsets):
    half_width = value_rows.shape[-1] // 2
    frequency = rope_base ** (
        -2.0 * jnp.arange(half_width, dtype=jnp.float32) / value_rows.shape[-1]
    )
    angles = offsets.astype(jnp.float32)[:, None] * frequency[None, :]
    cosine = jnp.cos(angles)[:, None, :]
    sine_table = jnp.sin(angles)[:, None, :]
    lower_half = value_rows[..., :half_width]
    upper_half = value_rows[..., half_width:]
    return jnp.concatenate(
        [
            lower_half * cosine - upper_half * sine_table,
            upper_half * cosine + lower_half * sine_table,
        ],
        axis=-1,
    )


def layout(segment, dealing):
    row_seg = jnp.take(segment, dealing)
    before = jnp.sum((segment[None, :] < row_seg[:, None]).astype(jnp.int32), axis=1)
    return (row_seg, dealing - before)


def attend(query, key_selected, value_selected, row_seg, dealing):
    scores = jnp.einsum("qhd,khd->hqk", query, key_selected, preferred_element_type=jnp.float32)
    allowed = (row_seg[:, None] == row_seg[None, :]) & (dealing[None, :] <= dealing[:, None])
    masked = jnp.where(allowed[None], scores, -1e30)
    row_peak = jnp.max(masked, axis=-1, keepdims=True)
    raw_weights = jnp.where(allowed[None], jnp.exp(masked - row_peak), 0.0)
    row_total = jnp.sum(raw_weights, axis=-1, keepdims=True)
    weights = (raw_weights / row_total).astype(jnp.bfloat16)
    attended = jnp.einsum(
        "hqk,khd->qhd", weights, value_selected, preferred_element_type=jnp.float32
    )
    return attended.astype(jnp.bfloat16).reshape(query.shape[0], -1)


def shards(
    tokens,
    seg_ids,
    deal,
    page_table,
    in_gain,
    w_query,
    key_projection_weight,
    value_projection_weight,
    q_gain,
    key_norm_gain,
    w_out,
    post_gain,
    final_gain,
    embed,
):
    own_tokens = tokens[0]
    rows_dev = own_tokens.shape[0]
    segment = seg_ids[0]
    dealing = deal[0]
    width_of_head = q_gain.shape[0]
    heads_local = w_query.shape[1] // width_of_head
    sequence_index = lax.axis_index("seq")
    own_start = sequence_index * rows_dev
    row_seg, offsets = layout(segment, dealing)
    normed_own = rows_scaled(own_tokens.astype(jnp.float32), in_gain).astype(jnp.bfloat16)
    normed_all = lax.all_gather(normed_own, "seq", axis=0, tiled=True)
    rows_of_pack = normed_all.shape[0]
    key_value_offsets = lax.dynamic_slice_in_dim(offsets, own_start, rows_dev, 0)
    query_full, key_full, value_full, out_full = (
        lax.all_gather(w_query, "grp", axis=0, tiled=True),
        lax.all_gather(key_projection_weight, "grp", axis=0, tiled=True),
        lax.all_gather(value_projection_weight, "grp", axis=0, tiled=True),
        lax.all_gather(w_out, "grp", axis=1, tiled=True),
    )
    query_raw = jnp.dot(normed_all, query_full, preferred_element_type=jnp.float32)
    key_unnormed = jnp.dot(normed_own, key_full, preferred_element_type=jnp.float32)
    value_unnormed = jnp.dot(normed_own, value_full, preferred_element_type=jnp.float32)
    query = rotate(
        rows_scaled(query_raw.reshape(rows_of_pack, heads_local, width_of_head), q_gain), offsets
    ).astype(jnp.bfloat16)
    rows_of_source = normed_own.shape[0]
    key_local_part = rotate(
        rows_scaled(key_unnormed.reshape(rows_of_source, KEY_HEADS, width_of_head), key_norm_gain),
        key_value_offsets,
    ).astype(jnp.bfloat16)
    value_local_part = rows_scaled(
        value_unnormed.reshape(rows_of_source, KEY_HEADS, width_of_head), 1.0
    ).astype(jnp.bfloat16)
    key_local_part = key_local_part.reshape(rows_of_source, KEY_HEADS * width_of_head)
    value_local_part = value_local_part.reshape(rows_of_source, KEY_HEADS * width_of_head)
    key_gathered, value_gathered = (
        lax.all_gather(key_local_part, "seq", axis=0, tiled=True),
        lax.all_gather(value_local_part, "seq", axis=0, tiled=True),
    )
    index_of_head = (sequence_index * heads_local + jnp.arange(heads_local, dtype=jnp.int32)) // (
        QUERY_HEADS // KEY_HEADS
    )
    key_selected = jnp.take(
        key_gathered.reshape(rows_of_pack, KEY_HEADS, width_of_head), index_of_head, axis=1
    )
    value_selected = jnp.take(
        value_gathered.reshape(rows_of_pack, KEY_HEADS, width_of_head), index_of_head, axis=1
    )
    attended = attend(query, key_selected, value_selected, row_seg, dealing)
    partial_out = jnp.dot(attended, out_full, preferred_element_type=jnp.float32)
    summed = lax.psum_scatter(
        partial_out.astype(jnp.bfloat16), "seq", scatter_dimension=0, tiled=True
    ).astype(jnp.float32)
    hidden = (own_tokens.astype(jnp.float32) + rows_scaled(summed, post_gain)).astype(jnp.bfloat16)
    inverse_assignment = jnp.argsort(dealing)
    inverse_page = jnp.argsort(page_table[0])
    own_pages = rows_dev // PAGE_SLOTS
    physical = sequence_index * own_pages + jnp.arange(own_pages, dtype=jnp.int32)
    logical_index = jnp.take(inverse_page, physical)
    packed = logical_index[:, None] * PAGE_SLOTS + jnp.arange(PAGE_SLOTS, dtype=jnp.int32)[None, :]
    source_index = jnp.take(inverse_assignment, packed.reshape(-1))
    stacked_rows = jnp.concatenate([key_gathered, value_gathered], axis=1)
    cache_pages = jnp.take(stacked_rows, source_index, axis=0).reshape(
        own_pages, PAGE_SLOTS, stacked_rows.shape[1]
    )
    last_pos = (
        jnp.sum(
            (segment[None, :] <= jnp.arange(SEGS, dtype=jnp.int32)[:, None]).astype(jnp.int32),
            axis=1,
        )
        - 1
    )
    local_row = jnp.take(inverse_assignment, last_pos) - own_start
    selector = (local_row[:, None] == jnp.arange(rows_dev, dtype=jnp.int32)[None, :]).astype(
        jnp.bfloat16
    )
    group_states = jnp.dot(selector, hidden, preferred_element_type=jnp.float32)
    pack_states = lax.psum(group_states.astype(jnp.bfloat16), "seq")
    states = lax.all_gather(pack_states, "grp", axis=0, tiled=True).astype(jnp.float32)
    last_norm = jnp.sqrt(jnp.mean(states * states, axis=-1))
    final = rows_scaled(states, final_gain).astype(jnp.bfloat16)
    logits = lax.dot_general(
        final, embed, (((1,), (1,)), ((), ())), preferred_element_type=jnp.float32
    )
    shard_max = jnp.max(cap_value * jnp.tanh(logits / cap_value), axis=1)
    max_logit = lax.pmax(shard_max, ("grp", "seq"))
    return (hidden[None], cache_pages[None], last_norm, max_logit)


def solution(mesh):
    return jax.shard_map(
        shards,
        mesh=mesh,
        in_specs=(
            P("grp", "seq", None),
            P("grp", None),
            P("grp", None),
            P("grp", None),
            P(),
            P("grp", "seq"),
            P("grp", None),
            P("grp", None),
            P(),
            P(),
            P("seq", "grp"),
            P(),
            P(),
            P(("grp", "seq"), None),
        ),
        out_specs=(P("grp", "seq", None), P("grp", "seq", None, None), P(), P()),
        check_vma=False,
    )
```

profile of v0, /device:TPU:1, one launch (start us, length us, event | category | flops | bytes accessed | tf_op | source)
XLA Modules:
  0.0 1011.3 jit_solution(3232940448721086610)
XLA Ops:
  9.5 5.7 gather_fusion
  16.3 132.1 %all-gather.18.cloned.1.call-done = bf16[2048,512]{1,0:T(8,128)(2,1)} async-done(((bf16[32,512]{1,0:T(8,128)(2,1)}), bf16[2048,512]{1,0:T(8,128)(2,1)}) %all-gather.18.cloned.1.call-update) | async-done | bytes 2097168 | tf_op jit(solution)/shard_map/all_gather | solution.py:90
  148.5 3.9 copy.40
  152.4 2.5 multiply_reduce_fusion.2
  156.1 132.3 %all-gather.10.cloned.1.call-done = bf16[2048,512]{1,0:T(8,128)(2,1)} async-done(((bf16[32,512]{1,0:T(8,128)(2,1)}), bf16[2048,512]{1,0:T(8,128)(2,1)}) %all-gather.10.cloned.1.call-update) | async-done | bytes 2097168 | tf_op jit(solution)/shard_map/all_gather | solution.py:91
  288.4 4.0 copy.36
  292.4 2.5 multiply_reduce_fusion.3
  298.6 29.0 %all-gather.20.cloned.1.call-done = bf16[1024,512]{1,0:T(8,128)(2,1)} async-done(((bf16[128,512]{1,0:T(8,128)(2,1)}), bf16[1024,512]{1,0:T(8,128)(2,1)}) %all-gather.20.cloned.1.call-update) | async-done | bytes 1048592 | tf_op jit(solution)/shard_map/all_gather | solution.py:111
  327.6 2.2 reshape.529
  329.8 3.3 constant_dynamic-slice_fusion
  333.1 27.5 %all-gather.12.cloned.1.call-done = bf16[1024,512]{1,0:T(8,128)(2,1)} async-done(((bf16[128,512]{1,0:T(8,128)(2,1)}), bf16[1024,512]{1,0:T(8,128)(2,1)}) %all-gather.12.cloned.1.call-update) | async-done | bytes 1048592 | tf_op jit(solution)/shard_map/all_gather | solution.py:112
  360.6 2.2 reshape.527
  362.8 3.3 constant_dynamic-slice_fusion.1
  366.1 126.2 %all-gather.16.cloned.1.call-done = bf16[2048,256]{1,0:T(8,128)(2,1)} async-done(((bf16[32,256]{1,0:T(8,128)(2,1)}), bf16[2048,256]{1,0:T(8,128)(2,1)}) %all-gather.16.cloned.1.call-update) | async-done | bytes 1048592 | tf_op jit(solution)/shard_map/all_gather | solution.py:89
  492.3 48.3 %all-gather.14.cloned.1.call-done = bf16[1024,2048]{1,0:T(8,128)(2,1)} async-done(((bf16[128,2048]{1,0:T(8,128)(2,1)}), bf16[1024,2048]{1,0:T(8,128)(2,1)}) %all-gather.14.cloned.1.call-update) | async-done | bytes 4194320 | tf_op jit(solution)/shard_map/all_gather | solution.py:85
  540.6 3.9 multiply_reduce_fusion.1
  544.7 2.3 fusion.46
  548.0 2.0 copy-done.3
  551.5 121.2 %all-gather.22.cloned.1.call-done = bf16[256,2048]{0,1:T(8,128)(2,1)} async-done(((bf16[256,32]{0,1:T(8,128)(2,1)}), bf16[256,2048]{0,1:T(8,128)(2,1)}) %all-gather.22.cloned.1.call-update) | async-done | bytes 1048592 | tf_op jit(solution)/shard_map/all_gather | solution.py:92
  672.7 7.6 convolution_convert_fusion
  680.4 4.4 sort.35
  684.8 2.5 sort.34
  688.8 40.6 %reduce-scatter.2.cloned.1.call-done = bf16[128,2048]{1,0:T(8,128)(2,1)} async-done(((bf16[1024,2048]{1,0:T(8,128)(2,1)}), bf16[128,2048]{1,0:T(8,128)(2,1)}) %reduce-scatter.2.cloned.1.call-update) | async-done | bytes 524304 | tf_op jit(solution)/shard_map/reduce_scatter | solution.py:125
  730.6 1.5 convolution_convert_fusion.1
  732.1 24.1 %psum.7 = bf16[4,2048]{1,0:T(4,128)(2,1)} all-reduce(bf16[4,2048]{1,0:T(4,128)(2,1)S(1)} %convolution_convert_fusion.1), channel_id=1, replica_groups=mesh['grp'=64,'seq'=8] {'seq'}, use_global_device_ids=true, to_apply=%region_12.14 | all-reduce | flops 8192 | bytes 32768 | tf_op jit(solution)/shard_map/psum | solution.py:152
  757.6 3.2 pad_maximum_fusion
  760.8 2.9 gather_fusion.3
  765.5 121.9 %all-gather.24.cloned.1.call-done = bf16[64,4,2048]{2,1,0:T(4,128)(2,1)} async-done(((bf16[1,4,2048]{2,1,0:T(4,128)(2,1)}), bf16[64,4,2048]{2,1,0:T(4,128)(2,1)}) %all-gather.24.cloned.1.call-update) | async-done | bytes 1048592 | tf_op jit(solution)/shard_map/all_gather | solution.py:153
  887.5 2.5 reshape.630
  890.0 1.8 multiply_reduce_fusion
  892.3 2.4 fusion.10
  894.8 110.0 %pmax.7 = f32[256]{0:T(256)} all-reduce(f32[256]{0:T(256)S(1)} %fusion.10), channel_id=1, replica_groups=mesh['grp'=64,'seq'=8] {'grp','seq'}, use_global_device_ids=true, to_apply=%region_15.17 | all-reduce | flops 256 | bytes 2048 | tf_op jit(solution)/shard_map/pmax | solution.py:160
  (94 shorter events, 17.3 us)
Async XLA Ops:
  7.2 885.2 %copy-start = (bf16[512,2048]{1,0:T(8,128)(2,1)S(1)}, bf16[512,2048]{1,0:T(8,128)(2,1)}, u32[]{:S(2)}) copy-start(bf16[512,2048]{1,0:T(8,128)(2,1)} %param.29) | copy-start | bytes 6291460
  7.2 8.0 copy-start.6
  7.2 8.1 copy-start.1
  7.2 8.6 copy-start.2
  7.2 141.2 %all-gather.18.cloned.1.call-start = ((), (), s32[]{:S(2)}) async-start(), calls=%async_computation.5 | async-start | bytes 2129920 | tf_op jit(solution)/shard_map/all_gather | solution.py:90
  7.9 280.5 %all-gather.10.cloned.1.call-start = ((), (), s32[]{:S(2)}) async-start(), calls=%async_computation.1 | async-start | bytes 2129920 | tf_op jit(solution)/shard_map/all_gather | solution.py:91
  8.7 318.9 %all-gather.20.cloned.1.call-start = ((), (), s32[]{:S(2)}) async-start(), calls=%async_computation.6 | async-start | bytes 1179648 | tf_op jit(solution)/shard_map/all_gather | solution.py:111
  9.4 143.0 %copy-start.7 = (f32[2048]{0:T(1024)S(1)}, f32[2048]{0:T(1024)}, u32[]{:S(2)}) copy-start(f32[2048]{0:T(1024)} %param.20) | copy-start | bytes 24580
  15.2 139.7 %copy-start.9 = (f32[256]{0:T(256)S(1)}, f32[256]{0:T(256)}, u32[]{:S(2)}) copy-start(f32[256]{0:T(256)} %param.25) | copy-start | bytes 3076
  156.0 204.6 %all-gather.12.cloned.1.call-start = ((), (), s32[]{:S(2)}) async-start(), calls=%async_computation.2 | async-start | bytes 1179648 | tf_op jit(solution)/shard_map/all_gather | solution.py:112
  295.9 196.3 %all-gather.16.cloned.1.call-start = ((), (), s32[]{:S(2)}) async-start(), calls=%async_computation.4 | async-start | bytes 1064960 | tf_op jit(solution)/shard_map/all_gather | solution.py:89
  296.5 244.1 %all-gather.14.cloned.1.call-start = ((), (), s32[]{:S(2)}) async-start(), calls=%async_computation.3 | async-start | bytes 4718592 | tf_op jit(solution)/shard_map/all_gather | solution.py:85
  297.6 375.1 %all-gather.22.cloned.1.call-start = ((), (), s32[]{:S(2)}) async-start(), calls=%async_computation.7 | async-start | bytes 1064960 | tf_op jit(solution)/shard_map/all_gather | solution.py:92
  298.3 431.1 %reduce-scatter.2.cloned.1.call-start = ((), (), s32[]{:S(2)}) async-start(), calls=%async_computation.8 | async-start | bytes 4718592 | tf_op jit(solution)/shard_map/reduce_scatter | solution.py:125
  366.1 178.5 %copy-start.10 = (f32[256]{0:T(256)S(1)}, f32[256]{0:T(256)}, u32[]{:S(2)}) copy-start(f32[256]{0:T(256)} %param.24) | copy-start | bytes 3076
  540.6 6.4 copy-start.5
  548.0 2.0 copy-start.3
  680.3 4.5 copy-start.12
  680.3 50.3 %copy-start.8 = (f32[2048]{0:T(1024)S(1)}, f32[2048]{0:T(1024)}, u32[]{:S(2)}) copy-start(f32[2048]{0:T(1024)} %param.27) | copy-start | bytes 24580
  680.3 207.2 %all-gather.24.cloned.1.call-start = ((), (), s32[]{:S(2)}) async-start(), calls=%async_computation.9 | async-start | bytes 1064960 | tf_op jit(solution)/shard_map/all_gather | solution.py:153
  730.6 33.9 %copy-start.4 = (bf16[128,2048]{1,0:T(8,128)(2,1)S(1)}, bf16[128,2048]{1,0:T(8,128)(2,1)}, u32[]{:S(2)}) copy-start(bf16[128,2048]{1,0:T(8,128)(2,1)} %reduce-scatter.2.cloned.1.call-done) | copy-start | bytes 1572868
  763.7 128.7 %copy-start.11 = (f32[2048]{0:T(1024)S(1)}, f32[2048]{0:T(1024)}, u32[]{:S(2)}) copy-start(f32[2048]{0:T(1024)} %param.28) | copy-start | bytes 24580
Sparse Core Ops, SparseCore 0:
  11.0 137.4 all-gather.17
  151.4 136.9 all-gather.9
  291.1 36.4 all-gather.19
  329.6 30.9 all-gather.11
  363.4 128.8 all-gather.15
  494.8 45.7 all-gather.13
  543.6 129.0 all-gather.21
  680.5 48.8 reduce-scatter.1
  756.3 131.0 all-gather.23
where the time goes:
time: 1010 us
  waiting for transfers between devices  782 us (77%)
  blocking collectives  134 us (13%)
  local copies, waits for them, and re-layouts  36.2 us (4%)
  other arithmetic  22.9 us (2%)
  matrix products  21.4 us (2%)
  between operations  14.2 us (1%)
    all_gather x1, waiting for transfers between devices, shards(): lax.all_gather(value_projection_weight, 'grp', axis=0, tiled=True)  132 us
    all_gather x1, waiting for transfers between devices, shards(): lax.all_gather(key_projection_weight, 'grp', axis=0, tiled=True)  132 us
    all_gather x1, waiting for transfers between devices, shards(): lax.all_gather(w_query, 'grp', axis=0, tiled=True)  126 us
    all_gather x1, waiting for transfers between devices, shards(): lax.all_gather(pack_states, 'grp', axis=0, tiled=True).astype(jnp.float32)  122 us
    all_gather x1, waiting for transfers between devices, shards(): lax.all_gather(w_out, 'grp', axis=1, tiled=True)  121 us
    pmax x1, blocking collectives, shards(): max_logit = lax.pmax(shard_max, ('grp', 'seq'))  110 us
    all_gather x1, waiting for transfers between devices, shards(): normed_all = lax.all_gather(normed_own, 'seq', axis=0, tiled=True)  48.3 us
    reduce_scatter x1, waiting for transfers between devices, shards(): lax.psum_scatter(partial_out.astype(jnp.bfloat16), 'seq', scatter_dimensi...  40.6 us
  transfers between devices with their start and end apart: 9, of which 9 were waited for; matrix products, arithmetic and copies ran while one was open for 6% of the time, Pallas kernels for 0%

commit v1 on v0

--- a/solution.py
+++ b/solution.py
@@ -85,10 +85,16 @@
     normed_all = lax.all_gather(normed_own, "seq", axis=0, tiled=True)
     rows_of_pack = normed_all.shape[0]
     key_value_offsets = lax.dynamic_slice_in_dim(offsets, own_start, rows_dev, 0)
+    classes_make = lambda panel: jnp.concatenate(
+        lax.all_to_all(
+            jnp.stack([panel] * lax.axis_size("grp")), split_axis=0, concat_axis=0, axis_name="grp"
+        ),
+        0,
+    )
     query_full, key_full, value_full, out_full = (
         lax.all_gather(w_query, "grp", axis=0, tiled=True),
         lax.all_gather(key_projection_weight, "grp", axis=0, tiled=True),
-        lax.all_gather(value_projection_weight, "grp", axis=0, tiled=True),
+        classes_make(value_projection_weight),
         lax.all_gather(w_out, "grp", axis=1, tiled=True),
     )
     query_raw = jnp.dot(normed_all, query_full, preferred_element_type=jnp.float32)

time: 1010 us -> 887 us (0.88)
  waiting for transfers between devices: 782 us -> 646 us
    all_gather x1 -> x0, waiting for transfers between devices: 132 us -> none  [shards(): lax.all_gather(value_projection_weight, 'grp', axis=0, tiled=True)]
    all_to_all x0 -> x1, waiting for transfers between devices: none -> 86.1 us  [shards(): lax.all_to_all(jnp.stack([panel] * lax.axis_size('grp')), split_axis=0, c...]
    all_gather x1, waiting for transfers between devices: 126 us -> 64.8 us  [shards(): lax.all_gather(w_query, 'grp', axis=0, tiled=True)]
    all_gather x1, waiting for transfers between devices: 29 us -> 0.02 us  [shards(): lax.all_gather(key_local_part, 'seq', axis=0, tiled=True)]
  transfers between devices with their start and end apart: 9 -> 9, of which waited for: 9 -> 8; matrix products, arithmetic and copies ran while one was open for 6% -> 6% of each run, Pallas kernels for 0% -> 0%
where the time goes in v1:
time: 887 us; the launch traced here: 886 us
  waiting for transfers between devices  646 us (73%)
  blocking collectives  134 us (15%)
  local copies, waits for them, and re-layouts  37.8 us (4%)
  other arithmetic  22.9 us (3%)
  matrix products  21.5 us (2%)
  between operations  14.6 us (2%)
  starting transfers between devices  9.58 us (1%)
    all_gather x1, waiting for transfers between devices, shards(): lax.all_gather(key_projection_weight, 'grp', axis=0, tiled=True)  133 us
    all_gather x1, waiting for transfers between devices, shards(): lax.all_gather(w_out, 'grp', axis=1, tiled=True)  126 us
    all_gather x1, waiting for transfers between devices, shards(): lax.all_gather(pack_states, 'grp', axis=0, tiled=True).astype(jnp.float32)  122 us
    pmax x1, blocking collectives, shards(): max_logit = lax.pmax(shard_max, ('grp', 'seq'))  110 us
    all_to_all x1, waiting for transfers between devices, shards(): lax.all_to_all(jnp.stack([panel] * lax.axis_size('grp')), split_axis=0, c...  86.1 us
    all_gather x1, waiting for transfers between devices, shards(): lax.all_gather(w_query, 'grp', axis=0, tiled=True)  64.8 us
    all_gather x1, waiting for transfers between devices, shards(): normed_all = lax.all_gather(normed_own, 'seq', axis=0, tiled=True)  48.3 us
    reduce_scatter x1, waiting for transfers between devices, shards(): lax.psum_scatter(partial_out.astype(jnp.bfloat16), 'seq', scatter_dimensi...  40.6 us
  transfers between devices with their start and end apart: 9, of which 8 were waited for; matrix products, arithmetic and copies ran while one was open for 6% of the time, Pallas kernels for 0%

profile of v1, /device:TPU:1, one launch (start us, length us, event | category | flops | bytes accessed | tf_op | source)
XLA Modules:
  0.0 885.9 jit_solution(2725317252822880056)
XLA Ops:
  8.7 5.7 gather_fusion
  15.6 132.9 %all-gather.15.cloned.1.call-done = bf16[2048,512]{1,0:T(8,128)(2,1)} async-done(((bf16[32,512]{1,0:T(8,128)(2,1)}), bf16[2048,512]{1,0:T(8,128)(2,1)}) %all-gather.15.cloned.1.call-update) | async-done | bytes 2097168 | tf_op jit(solution)/shard_map/all_gather | solution.py:96
  148.5 4.0 copy.40
  152.4 2.5 multiply_reduce_fusion.2
  156.8 1.6 stack.2
  158.4 9.1 %all-to-all-start = ((bf16[64,32,512]{2,1,0:T(8,128)(2,1)}), bf16[64,32,512]{2,1,0:T(8,128)(2,1)}, u32[]{:S(2)}, u32[]{:S(2)}) async-start(bf16[64,32,512]{2,1,0:T(8,128)(2,1)} %stack.2), calls=%async_computation | async-start | bytes 4194304 | tf_op jit(solution)/shard_map/all_to_all | solution.py:89
  168.6 86.1 %all-to-all-done = bf16[64,32,512]{2,1,0:T(8,128)(2,1)} async-done(((bf16[64,32,512]{2,1,0:T(8,128)(2,1)}), bf16[64,32,512]{2,1,0:T(8,128)(2,1)}, u32[]{:S(2)}, u32[]{:S(2)}) %all-to-all-start) | async-done | bytes 2097184 | tf_op jit(solution)/shard_map/all_to_all | solution.py:89
  254.7 4.0 copy.36
  258.7 2.5 multiply_reduce_fusion.3
  263.1 2.2 reshape.535
  265.3 3.3 constant_dynamic-slice_fusion
  268.6 64.8 %all-gather.13.cloned.1.call-done = bf16[2048,256]{1,0:T(8,128)(2,1)} async-done(((bf16[32,256]{1,0:T(8,128)(2,1)}), bf16[2048,256]{1,0:T(8,128)(2,1)}) %all-gather.13.cloned.1.call-update) | async-done | bytes 1048592 | tf_op jit(solution)/shard_map/all_gather | solution.py:95
  333.5 48.3 %all-gather.11.cloned.1.call-done = bf16[1024,2048]{1,0:T(8,128)(2,1)} async-done(((bf16[128,2048]{1,0:T(8,128)(2,1)}), bf16[1024,2048]{1,0:T(8,128)(2,1)}) %all-gather.11.cloned.1.call-update) | async-done | bytes 4194320 | tf_op jit(solution)/shard_map/all_gather | solution.py:85
  381.8 3.9 multiply_reduce_fusion.1
  385.9 2.3 fusion.46
  389.2 1.9 copy-done.3
  392.6 22.4 %all-gather.9.cloned.1.call-done = bf16[1024,512]{1,0:T(8,128)(2,1)} async-done(((bf16[128,512]{1,0:T(8,128)(2,1)}), bf16[1024,512]{1,0:T(8,128)(2,1)}) %all-gather.9.cloned.1.call-update) | async-done | bytes 1048592 | tf_op jit(solution)/shard_map/all_gather | solution.py:118
  415.1 2.1 reshape.533
  417.2 3.3 constant_dynamic-slice_fusion.1
  420.5 126.2 %all-gather.19.cloned.1.call-done = bf16[256,2048]{0,1:T(8,128)(2,1)} async-done(((bf16[256,32]{0,1:T(8,128)(2,1)}), bf16[256,2048]{0,1:T(8,128)(2,1)}) %all-gather.19.cloned.1.call-update) | async-done | bytes 1048592 | tf_op jit(solution)/shard_map/all_gather | solution.py:98
  546.7 7.6 convolution_convert_fusion
  554.5 4.4 sort.35
  558.8 2.5 sort.34
  562.8 40.6 %reduce-scatter.2.cloned.1.call-done = bf16[128,2048]{1,0:T(8,128)(2,1)} async-done(((bf16[1024,2048]{1,0:T(8,128)(2,1)}), bf16[128,2048]{1,0:T(8,128)(2,1)}) %reduce-scatter.2.cloned.1.call-update) | async-done | bytes 524304 | tf_op jit(solution)/shard_map/reduce_scatter | solution.py:131
  606.2 24.1 %psum.7 = bf16[4,2048]{1,0:T(4,128)(2,1)} all-reduce(bf16[4,2048]{1,0:T(4,128)(2,1)S(1)} %convolution_convert_fusion.1), channel_id=1, replica_groups=mesh['grp'=64,'seq'=8] {'seq'}, use_global_device_ids=true, to_apply=%region_12.14 | all-reduce | flops 8192 | bytes 32768 | tf_op jit(solution)/shard_map/psum | solution.py:158
  631.7 3.2 pad_maximum_fusion
  634.8 2.9 gather_fusion.3
  639.6 122.1 %all-gather.21.cloned.1.call-done = bf16[64,4,2048]{2,1,0:T(4,128)(2,1)} async-done(((bf16[1,4,2048]{2,1,0:T(4,128)(2,1)}), bf16[64,4,2048]{2,1,0:T(4,128)(2,1)}) %all-gather.21.cloned.1.call-update) | async-done | bytes 1048592 | tf_op jit(solution)/shard_map/all_gather | solution.py:159
  761.7 2.5 reshape.636
  764.2 1.8 multiply_reduce_fusion
  766.6 2.4 fusion.10
  769.0 110.0 %pmax.7 = f32[256]{0:T(256)} all-reduce(f32[256]{0:T(256)S(1)} %fusion.10), channel_id=1, replica_groups=mesh['grp'=64,'seq'=8] {'grp','seq'}, use_global_device_ids=true, to_apply=%region_15.17 | all-reduce | flops 256 | bytes 2048 | tf_op jit(solution)/shard_map/pmax | solution.py:166
  (96 shorter events, 18.0 us)
Async XLA Ops:
  7.2 759.4 %copy-start = (bf16[512,2048]{1,0:T(8,128)(2,1)S(1)}, bf16[512,2048]{1,0:T(8,128)(2,1)}, u32[]{:S(2)}) copy-start(bf16[512,2048]{1,0:T(8,128)(2,1)} %param.29) | copy-start | bytes 6291460
  7.2 7.3 copy-start.6
  7.2 7.3 copy-start.1
  7.2 7.9 copy-start.2
  7.2 141.2 %all-gather.15.cloned.1.call-start = ((), (), s32[]{:S(2)}) async-start(), calls=%async_computation.5 | async-start | bytes 2129920 | tf_op jit(solution)/shard_map/all_gather | solution.py:96
  7.9 255.2 %all-gather.17.cloned.1.call-start = ((), (), s32[]{:S(2)}) async-start(), calls=%async_computation.6 | async-start | bytes 1179648 | tf_op jit(solution)/shard_map/all_gather | solution.py:117
  8.7 143.7 %copy-start.8 = (f32[2048]{0:T(1024)S(1)}, f32[2048]{0:T(1024)}, u32[]{:S(2)}) copy-start(f32[2048]{0:T(1024)} %param.20) | copy-start | bytes 24580
  14.4 140.5 %copy-start.10 = (f32[256]{0:T(256)S(1)}, f32[256]{0:T(256)}, u32[]{:S(2)}) copy-start(f32[256]{0:T(256)} %param.25) | copy-start | bytes 3076
  148.5 8.4 copy-start.7
  156.1 177.4 %all-gather.13.cloned.1.call-start = ((), (), s32[]{:S(2)}) async-start(), calls=%async_computation.4 | async-start | bytes 1064960 | tf_op jit(solution)/shard_map/all_gather | solution.py:95
  158.4 96.3 %all-to-all-start = ((bf16[64,32,512]{2,1,0:T(8,128)(2,1)}), bf16[64,32,512]{2,1,0:T(8,128)(2,1)}, u32[]{:S(2)}, u32[]{:S(2)}) async-start(bf16[64,32,512]{2,1,0:T(8,128)(2,1)} %stack.2), calls=%async_computation | async-start | bytes 4194304 | tf_op jit(solution)/shard_map/all_to_all | solution.py:89
  167.5 214.3 %all-gather.11.cloned.1.call-start = ((), (), s32[]{:S(2)}) async-start(), calls=%async_computation.3 | async-start | bytes 4718592 | tf_op jit(solution)/shard_map/all_gather | solution.py:85
  168.6 246.5 %all-gather.9.cloned.1.call-start = ((), (), s32[]{:S(2)}) async-start(), calls=%async_computation.2 | async-start | bytes 1179648 | tf_op jit(solution)/shard_map/all_gather | solution.py:118
  262.3 284.5 %all-gather.19.cloned.1.call-start = ((), (), s32[]{:S(2)}) async-start(), calls=%async_computation.7 | async-start | bytes 1064960 | tf_op jit(solution)/shard_map/all_gather | solution.py:98
  262.8 340.6 %reduce-scatter.2.cloned.1.call-start = ((), (), s32[]{:S(2)}) async-start(), calls=%async_computation.8 | async-start | bytes 4718592 | tf_op jit(solution)/shard_map/reduce_scatter | solution.py:131
  268.6 117.1 %copy-start.11 = (f32[256]{0:T(256)S(1)}, f32[256]{0:T(256)}, u32[]{:S(2)}) copy-start(f32[256]{0:T(256)} %param.24) | copy-start | bytes 3076
  381.8 6.4 copy-start.5
  389.2 1.9 copy-start.3
  554.4 4.5 copy-start.13
  554.4 50.3 %copy-start.9 = (f32[2048]{0:T(1024)S(1)}, f32[2048]{0:T(1024)}, u32[]{:S(2)}) copy-start(f32[2048]{0:T(1024)} %param.27) | copy-start | bytes 24580
  554.4 207.3 %all-gather.21.cloned.1.call-start = ((), (), s32[]{:S(2)}) async-start(), calls=%async_computation.9 | async-start | bytes 1064960 | tf_op jit(solution)/shard_map/all_gather | solution.py:159
  604.7 33.9 %copy-start.4 = (bf16[128,2048]{1,0:T(8,128)(2,1)S(1)}, bf16[128,2048]{1,0:T(8,128)(2,1)}, u32[]{:S(2)}) copy-start(bf16[128,2048]{1,0:T(8,128)(2,1)} %reduce-scatter.2.cloned.1.call-done) | copy-start | bytes 1572868
  637.7 128.8 %copy-start.12 = (f32[2048]{0:T(1024)S(1)}, f32[2048]{0:T(1024)}, u32[]{:S(2)}) copy-start(f32[2048]{0:T(1024)} %param.28) | copy-start | bytes 24580
Sparse Core Ops, SparseCore 0:
  11.0 137.4 all-gather.14
  156.2 36.2 all-gather.16
  195.5 137.9 all-gather.12
  336.0 45.7 all-gather.10
  383.8 31.2 all-gather.8
  417.9 128.8 all-gather.18
  554.5 48.8 reduce-scatter.1
  630.4 131.2 all-gather.20
